TPU v7x, 256 devices: a whole 4x4x8 slice. The times are simulated.
256 devices in a mesh: ha: 8 (over z_lo, core), wa: 32 (over y, x, z_hi).
Axes of the slice: x: 4, y: 4, z: 8 (z_hi: 2, z_lo: 4; z = z_hi * 4 + z_lo), core: 2. Of those that a mesh axis runs over, the one named last changes fastest.
Arguments:
- tokens: bfloat16 [1, 8, 64, 64, 1152], P(None, None, 'ha', 'wa'), may hold values from -36 to 36
- cotangent: bfloat16 [1, 8, 64, 64, 1152], P(None, None, 'ha', 'wa'), may hold values from -6 to 6
- w_qkv: bfloat16 [3, 1152, 1728], P(None, 'wa'), may hold values from -0.1875 to 0.1875
- w_out: bfloat16 [3, 576, 1152], P(None, 'wa'), may hold values from -0.25 to 0.25
- gains: float32 [3, 1152], replicated, may hold values from 0.1 to 1.9
- gates: float32 [3, 8], replicated, may hold values from 0.5 to 2
Outputs:
- token_grad: bfloat16 [1, 8, 64, 64, 1152], P(None, None, 'ha', 'wa')
- head_sens: bfloat16 [1, 3, 8, 64, 64, 8], P(None, None, None, 'ha', 'wa')
All inputs are finite; a program needn't handle non-finite values.
Results may differ from a plain program's by a relative error of at most 0.02.
Values may be sent and summed in bfloat16 or wider, within the bound.
A program may use at most 128 MiB of HBM per device.

v0:
```python
import jax
import jax.numpy as jnp
from jax import lax
from jax.sharding import PartitionSpec as P


def letter_forms(attend_axis):
    letters = "bfhw"
    query_side = letters + "nc"
    key_side = letters[:attend_axis] + "g" + letters[attend_axis + 1 :] + "nc"
    score_side = (
        letters[:attend_axis] + letters[attend_axis + 1 :] + "n" + letters[attend_axis] + "g"
    )
    return (
        query_side + "," + key_side + "->" + score_side,
        score_side + "," + key_side + "->" + query_side,
        score_side + "," + query_side + "->" + key_side,
    )


def product(form, left, right):
    return jnp.einsum(form, left, right, preferred_element_type=jnp.float32)


def forward_sublayer(inputs, w_qkv, w_out, gain, gate, attend_axis, keep_output):
    scores_form, mixing_form, keyward_form = letter_forms(attend_axis)
    heads = gate.shape[0]
    hidden = w_out.shape[0]
    head_dim = hidden // heads
    leading = inputs.shape[:4]
    inputs_f = inputs.astype(jnp.float32)
    inverse = lax.rsqrt(jnp.mean(inputs_f * inputs_f, axis=-1, keepdims=True) + 1e-06)
    normed = (inputs_f * inverse * gain).astype(jnp.bfloat16)
    projected = jnp.dot(normed, w_qkv, preferred_element_type=jnp.float32).astype(jnp.bfloat16)
    split = projected.reshape(leading + (3, heads, head_dim))
    queries = split[..., 0, :, :]
    keys_all = split[..., 1, :, :]
    values = split[..., 2, :, :]
    scores = product(scores_form, queries, keys_all) * head_dim ** (-0.5)
    raised = jnp.exp(scores)
    probs = raised / jnp.sum(raised, axis=-1, keepdims=True)
    probs_half = probs.astype(jnp.bfloat16)
    attended = product(mixing_form, probs_half, values).astype(jnp.bfloat16)
    saved = (inverse, queries, keys_all, values, probs, probs_half, attended)
    if not keep_output:
        return (inputs, saved)
    gated = (
        (attended.astype(jnp.float32) * gate[:, None])
        .astype(jnp.bfloat16)
        .reshape(leading + (hidden,))
    )
    outputs = (inputs_f + jnp.dot(gated, w_out, preferred_element_type=jnp.float32)).astype(
        jnp.bfloat16
    )
    return (outputs, saved)


def backward_sublayer(outgrad, inputs, saved, w_qkv, w_out, gain, gate, attend_axis):
    scores_form, mixing_form, keyward_form = letter_forms(attend_axis)
    inverse, queries, keys_all, values, probs, probs_half, attended = saved
    heads = gate.shape[0]
    hidden = w_out.shape[0]
    head_dim = hidden // heads
    leading = inputs.shape[:4]
    d_gated = jnp.dot(outgrad, w_out.T, preferred_element_type=jnp.float32).astype(jnp.bfloat16)
    d_gated = d_gated.reshape(leading + (heads, head_dim))
    sens = jnp.sum(d_gated.astype(jnp.float32) * attended.astype(jnp.float32), axis=-1).astype(
        jnp.bfloat16
    )
    d_attended = (d_gated.astype(jnp.float32) * gate[:, None]).astype(jnp.bfloat16)
    d_probs = product(scores_form, d_attended, values)
    d_values = product(keyward_form, probs_half, d_attended)
    d_scores = (
        probs * (d_probs - jnp.sum(d_probs * probs, axis=-1, keepdims=True)) * head_dim ** (-0.5)
    ).astype(jnp.bfloat16)
    d_queries = product(mixing_form, d_scores, keys_all)
    d_keys = product(keyward_form, d_scores, queries)
    d_proj = (
        jnp.stack([d_queries, d_keys, d_values], axis=4)
        .reshape(leading + (3 * hidden,))
        .astype(jnp.bfloat16)
    )
    d_normed = jnp.dot(d_proj, w_qkv.T, preferred_element_type=jnp.float32) * gain
    inputs_f = inputs.astype(jnp.float32)
    ingrad = (
        outgrad.astype(jnp.float32)
        + inverse * d_normed
        - inputs_f
        * inverse
        * inverse
        * inverse
        * jnp.mean(inputs_f * d_normed, axis=-1, keepdims=True)
    )
    return (ingrad.astype(jnp.bfloat16), sens)


def per_device(tokens, cotangent, w_qkv, w_out, gains, gates):
    heads = gates.shape[1]

    def weights_for(sublayer):
        return (
            lax.all_gather(w_qkv[sublayer], "wa", axis=0, tiled=True),
            lax.all_gather(w_out[sublayer], "wa", axis=0, tiled=True),
        )

    qkv_first, out_first = weights_for(0)
    after_time, saved_time = forward_sublayer(
        tokens, qkv_first, out_first, gains[0], gates[0], 1, True
    )
    qkv_second, out_second = weights_for(1)
    tall_input = lax.all_to_all(after_time, "ha", split_axis=1, concat_axis=2, tiled=True)
    after_height, saved_height = forward_sublayer(
        tall_input, qkv_second, out_second, gains[1], gates[1], 2, True
    )
    qkv_third, out_third = weights_for(2)
    wide_input = lax.all_to_all(after_height, "wa", split_axis=2, concat_axis=3, tiled=True)
    wide_same, saved_width = forward_sublayer(
        wide_input, qkv_third, out_third, gains[2], gates[2], 3, False
    )
    tall_cot = lax.all_to_all(cotangent, "ha", split_axis=1, concat_axis=2, tiled=True)
    wide_cot = lax.all_to_all(tall_cot, "wa", split_axis=2, concat_axis=3, tiled=True)
    grad_width, sens_width = backward_sublayer(
        wide_cot, wide_input, saved_width, qkv_third, out_third, gains[2], gates[2], 3
    )
    tall_grad, tall_sens = (
        lax.all_to_all(grad_width, "wa", split_axis=3, concat_axis=2, tiled=True),
        lax.all_to_all(sens_width, "wa", split_axis=3, concat_axis=2, tiled=True),
    )
    grad_height, sens_height = backward_sublayer(
        tall_grad, tall_input, saved_height, qkv_second, out_second, gains[1], gates[1], 2
    )
    home_cot, both_sens = (
        lax.all_to_all(grad_height, "ha", split_axis=2, concat_axis=1, tiled=True),
        lax.all_to_all(
            jnp.concatenate([tall_sens, sens_height], axis=-1),
            "ha",
            split_axis=2,
            concat_axis=1,
            tiled=True,
        ),
    )
    home_sens_width = both_sens[..., :heads]
    home_sens_height = both_sens[..., heads:]
    token_grad, sens_time = backward_sublayer(
        home_cot, tokens, saved_time, qkv_first, out_first, gains[0], gates[0], 1
    )
    head_sens = jnp.stack([sens_time, home_sens_height, home_sens_width], axis=1)
    return (token_grad, head_sens)


def solution(mesh):
    in_specs = (
        P(None, None, "ha", "wa", None),
        P(None, None, "ha", "wa", None),
        P(None, "wa", None),
        P(None, "wa", None),
        P(),
        P(),
    )
    out_specs = (P(None, None, "ha", "wa", None), P(None, None, None, "ha", "wa", None))
    return jax.shard_map(
        per_device, mesh=mesh, in_specs=in_specs, out_specs=out_specs, check_vma=False
    )
```

profile of v0, /device:TPU:32, one launch (start us, length us, event | category | flops | bytes accessed | tf_op | source)
XLA Modules:
  0.0 883.0 jit_solution(4877952526610603117)
XLA Ops:
  14.5 6.0 all-to-all-start
  21.3 144.8 %all-gather.13.cloned.1.call-done = bf16[1,1152,1728]{2,0,1:T(2,128)(2,1)} async-done(((bf16[1,36,1728]{2,0,1:T(2,128)(2,1)}), bf16[1,1152,1728]{2,0,1:T(2,128)(2,1)}) %all-gather.13.cloned.1.call-update) | async-done | bytes 3981328 | tf_op jit(solution)/shard_map/all_gather | solution.py:102
  166.0 17.9 %copy.441 = bf16[1,1152,1728]{1,2,0:T(8,128)(2,1)} copy(bf16[1,1152,1728]{2,0,1:T(2,128)(2,1)} %all-gather.13.cloned.1.call-done) | data formatting | bytes 7962624 | tf_op jit(solution)/shard_map/all_gather | solution.py:102
  183.9 3.4 fusion.31
  188.9 1.2 multiply_convert_fusion.2
  190.3 70.8 %all-gather.15.cloned.1.call-done = bf16[1,576,1152]{2,0,1:T(2,128)(2,1)} async-done(((bf16[1,18,1152]{2,0,1:T(2,128)(2,1)}), bf16[1,576,1152]{2,0,1:T(2,128)(2,1)}) %all-gather.15.cloned.1.call-update) | async-done | bytes 1327120 | tf_op jit(solution)/shard_map/all_gather | solution.py:103
  261.1 2.9 fusion.37
  264.0 4.6 all-to-all-start.2
  268.6 142.1 %all-gather.17.cloned.1.call-done = bf16[1,1152,1728]{2,0,1:T(2,128)(2,1)} async-done(((bf16[1,36,1728]{2,0,1:T(2,128)(2,1)}), bf16[1,1152,1728]{2,0,1:T(2,128)(2,1)}) %all-gather.17.cloned.1.call-update) | async-done | bytes 3981328 | tf_op jit(solution)/shard_map/all_gather | solution.py:102
  410.7 17.8 %copy.453 = bf16[1,1152,1728]{1,2,0:T(8,128)(2,1)} copy(bf16[1,1152,1728]{2,0,1:T(2,128)(2,1)} %all-gather.17.cloned.1.call-done) | data formatting | bytes 7962624 | tf_op jit(solution)/shard_map/all_gather | solution.py:102
  428.5 6.1 all-to-all-start.1
  434.8 3.4 fusion.25
  441.1 64.0 %all-gather.19.cloned.1.call-done = bf16[1,576,1152]{2,0,1:T(2,128)(2,1)} async-done(((bf16[1,18,1152]{2,0,1:T(2,128)(2,1)}), bf16[1,576,1152]{2,0,1:T(2,128)(2,1)}) %all-gather.19.cloned.1.call-update) | async-done | bytes 1327120 | tf_op jit(solution)/shard_map/all_gather | solution.py:103
  505.1 2.2 fusion.36
  508.3 5.4 all-to-all-start.3
  513.7 1.2 copy.438
  515.0 84.1 %all-gather.23.cloned.1.call-done = bf16[1,576,1152]{2,0,1:T(2,128)(2,1)} async-done(((bf16[1,18,1152]{2,0,1:T(2,128)(2,1)}), bf16[1,576,1152]{2,0,1:T(2,128)(2,1)}) %all-gather.23.cloned.1.call-update) | async-done | bytes 1327120 | tf_op jit(solution)/shard_map/all_gather | solution.py:103
  599.1 2.3 fusion.91
  602.8 145.7 %all-gather.21.cloned.1.call-done = bf16[1,1152,1728]{2,0,1:T(2,128)(2,1)} async-done(((bf16[1,36,1728]{2,0,1:T(2,128)(2,1)}), bf16[1,1152,1728]{2,0,1:T(2,128)(2,1)}) %all-gather.21.cloned.1.call-update) | async-done | bytes 3981328 | tf_op jit(solution)/shard_map/all_gather | solution.py:102
  748.5 17.8 %copy.465 = bf16[1,1152,1728]{1,2,0:T(8,128)(2,1)} copy(bf16[1,1152,1728]{2,0,1:T(2,128)(2,1)} %all-gather.21.cloned.1.call-done) | data formatting | bytes 7962624 | tf_op jit(solution)/shard_map/all_gather | solution.py:102
  767.4 4.2 fusion.28
  771.7 2.0 reshape.545
  774.6 1.3 fusion.153
  776.0 1.7 fusion.167
  778.5 1.6 fusion.68
  780.2 1.5 fusion.69
  781.7 2.1 fusion.81
  783.8 1.4 copy.488
  785.2 6.1 all-to-all-start.6
  792.5 3.0 multiply_reduce_fusion.3
  796.9 6.4 all-to-all-done.6
  803.3 5.7 all-to-all-start.4
  809.9 12.6 %all-to-all-done.4 = bf16[1,1,2,64,1152]{4,2,1,0,3:T(2,128)(2,1)S(1)} async-done(((bf16[1,1,2,64,1152]{4,2,1,0,3:T(2,128)(2,1)}), bf16[1,1,2,64,1152]{4,2,1,0,3:T(2,128)(2,1)S(1)}, u32[]{:S(2)}, u32[]{:S(2)}) %all-to-all-start.4) | async-done | bytes 294944 | tf_op jit(solution)/shard_map/all_to_all | solution.py:126
  823.5 3.1 fusion.85
  826.7 1.2 reshape.554
  827.9 2.0 reshape.558
  829.9 1.1 fusion.166
  831.4 1.6 fusion.71
  833.0 1.5 fusion.72
  834.5 1.3 fusion.132
  836.6 6.8 all-to-all-start.7
  844.7 3.0 fusion.128
  849.0 5.1 all-to-all-start.5
  854.5 7.9 all-to-all-done.5
  863.1 2.3 fusion.97
  867.0 1.4 fusion.74
  868.4 1.4 fusion.75
  871.9 3.0 fusion.131
  (156 shorter events, 32.1 us)
Async XLA Ops:
  7.2 13.3 %copy-start.21 = (f32[3,1152]{1,0:T(4,128)S(1)}, f32[3,1152]{1,0:T(4,128)}, u32[]{:S(2)}) copy-start(f32[3,1152]{1,0:T(4,128)} %param.10) | copy-start | bytes 41476
  7.2 13.4 %copy-start = (bf16[1,8,8,2,1152]{4,3,2,1,0:T(2,128)(2,1)S(1)}, bf16[1,8,8,2,1152]{4,3,2,1,0:T(2,128)(2,1)}, u32[]{:S(2)}) copy-start(bf16[1,8,8,2,1152]{4,3,2,1,0:T(2,128)(2,1)} %param.6) | copy-start | bytes 884740
  7.2 13.5 %copy-start.30 = (f32[3,8]{1,0:T(4,128)S(1)}, f32[3,8]{1,0:T(4,128)}, u32[]{:S(2)}) copy-start(f32[3,8]{1,0:T(4,128)} %param.11) | copy-start | bytes 292
  7.2 158.8 %all-gather.13.cloned.1.call-start = ((), (), s32[]{:S(2)}) async-start(), calls=%async_computation.8 | async-start | bytes 8515584 | tf_op jit(solution)/shard_map/all_gather | solution.py:102
  9.3 251.9 %all-gather.15.cloned.1.call-start = ((), (), s32[]{:S(2)}) async-start(), calls=%async_computation.9 | async-start | bytes 2737152 | tf_op jit(solution)/shard_map/all_gather | solution.py:103
  10.9 399.7 %all-gather.17.cloned.1.call-start = ((), (), s32[]{:S(2)}) async-start(), calls=%async_computation.10 | async-start | bytes 8515584 | tf_op jit(solution)/shard_map/all_gather | solution.py:102
  12.0 493.1 %all-gather.19.cloned.1.call-start = ((), (), s32[]{:S(2)}) async-start(), calls=%async_computation.11 | async-start | bytes 2737152 | tf_op jit(solution)/shard_map/all_gather | solution.py:103
  12.7 586.4 %all-gather.23.cloned.1.call-start = ((), (), s32[]{:S(2)}) async-start(), calls=%async_computation.13 | async-start | bytes 2737152 | tf_op jit(solution)/shard_map/all_gather | solution.py:103
  13.5 735.0 %all-gather.21.cloned.1.call-start = ((), (), s32[]{:S(2)}) async-start(), calls=%async_computation.12 | async-start | bytes 8515584 | tf_op jit(solution)/shard_map/all_gather | solution.py:102
  14.5 249.5 %all-to-all-start = ((bf16[1,8,8,2,1152]{4,3,2,0,1:T(2,128)(2,1)}), bf16[1,8,8,2,1152]{4,3,2,0,1:T(2,128)(2,1)}, u32[]{:S(2)}, u32[]{:S(2)}) async-start(bf16[1,8,8,2,1152]{4,3,2,0,1:T(2,128)(2,1)} %bitcast.371), calls=%async_computation | async-start | bytes 589824 | tf_op jit(solution)/shard_map/all_to_all | solution.py:120
  20.5 163.4 %copy-start.19 = (f32[1152]{0:T(1024)}, f32[1152]{0:T(1024)S(1)}, u32[]{:S(2)}) copy-start(f32[1152]{0:T(1024)S(1)} %get-tuple-element.21) | copy-start | bytes 13828
  21.2 167.7 %copy-start.26 = (f32[8]{0:T(128)}, f32[8]{0:T(128)S(1)}, u32[]{:S(2)}) copy-start(f32[8]{0:T(128)S(1)} %get-tuple-element.41) | copy-start | bytes 100
  21.3 162.6 %copy-start.17 = (f32[8,8,2]{1,2,0:T(2,128)}, f32[8,8,2]{1,2,0:T(2,128)S(1)}, u32[]{:S(2)}) copy-start(f32[8,8,2]{1,2,0:T(2,128)S(1)} %add_rsqrt_fusion.2) | copy-start | bytes 1540
  188.4 1.7 copy-start.13
  188.4 75.6 %copy-start.14 = (bf16[1,8,8,2,1,8,72]{6,5,4,2,3,1,0:T(8,128)(2,1)}, bf16[1,8,8,2,1,8,72]{6,5,4,2,3,1,0:T(8,128)(2,1)S(1)}, u32[]{:S(2)}) copy-start(bf16[1,8,8,2,1,8,72]{6,5,4,2,3,1,0:T(8,128)(2,1)S(1)} %get-tuple-element.31) | copy-start | bytes 442372
  264.0 164.5 %all-to-all-start.2 = ((bf16[1,8,8,2,1152]{4,2,3,0,1:T(8,128)(2,1)}), bf16[1,8,8,2,1152]{4,2,3,0,1:T(8,128)(2,1)S(1)}, u32[]{:S(2)}, u32[]{:S(2)}) async-start(bf16[1,8,8,2,1152]{4,2,3,0,1:T(8,128)(2,1)} %fusion.37), calls=%async_computation.2 | async-start | bytes 589824 | tf_op jit(solution)/shard_map/all_to_all | solution.py:111
  428.5 79.8 %all-to-all-start.1 = ((bf16[1,1,64,2,1152]{4,3,1,0,2:T(2,128)(2,1)}), bf16[1,1,64,2,1152]{4,3,1,0,2:T(2,128)(2,1)}, u32[]{:S(2)}, u32[]{:S(2)}) async-start(bf16[1,1,64,2,1152]{4,3,1,0,2:T(2,128)(2,1)} %bitcast.2), calls=%async_computation.1 | async-start | bytes 589824 | tf_op jit(solution)/shard_map/all_to_all | solution.py:121
  434.8 3.4 copy-start.24
  438.2 1.4 copy-start.28
  439.2 69.1 %copy-start.1 = (bf16[1,1,64,2,1,8,72]{6,5,4,2,3,1,0:T(8,128)(2,1)}, bf16[1,1,64,2,1,8,72]{6,5,4,2,3,1,0:T(8,128)(2,1)S(1)}, u32[]{:S(2)}) copy-start(bf16[1,1,64,2,1,8,72]{6,5,4,2,3,1,0:T(8,128)(2,1)S(1)} %get-tuple-element.26) | copy-start | bytes 442372
  439.2 69.1 %copy-start.15 = (bf16[1,1,64,2,1,8,72]{6,5,4,2,3,1,0:T(8,128)(2,1)}, bf16[1,1,64,2,1,8,72]{6,5,4,2,3,1,0:T(8,128)(2,1)S(1)}, u32[]{:S(2)}) copy-start(bf16[1,1,64,2,1,8,72]{6,5,4,2,3,1,0:T(8,128)(2,1)S(1)} %get-tuple-element.27) | copy-start | bytes 442372
  439.2 69.1 %copy-start.16 = (bf16[1,1,64,2,1,8,72]{6,5,4,2,3,1,0:T(8,128)(2,1)}, bf16[1,1,64,2,1,8,72]{6,5,4,2,3,1,0:T(8,128)(2,1)S(1)}, u32[]{:S(2)}) copy-start(bf16[1,1,64,2,1,8,72]{6,5,4,2,3,1,0:T(8,128)(2,1)S(1)} %get-tuple-element.28) | copy-start | bytes 442372
  439.5 68.7 %copy-start.3 = (f32[2,8,64,64]{2,3,1,0:T(8,128)}, f32[2,8,64,64]{2,3,1,0:T(8,128)S(1)}, u32[]{:S(2)}) copy-start(f32[2,8,64,64]{2,3,1,0:T(8,128)S(1)} %fusion.155) | copy-start | bytes 786436
  508.3 258.0 %all-to-all-start.3 = ((bf16[1,1,64,2,1152]{4,3,1,0,2:T(2,128)(2,1)}), bf16[1,1,64,2,1152]{4,3,1,0,2:T(2,128)(2,1)S(1)}, u32[]{:S(2)}, u32[]{:S(2)}) async-start(bf16[1,1,64,2,1152]{4,3,1,0,2:T(2,128)(2,1)} %copy.460), calls=%async_computation.3 | async-start | bytes 589824 | tf_op jit(solution)/shard_map/all_to_all | solution.py:116
  515.0 251.3 %copy-start.7 = (bf16[2,64,1152]{2,1,0:T(8,128)(2,1)}, bf16[2,64,1152]{2,1,0:T(8,128)(2,1)S(1)}, u32[]{:S(2)}) copy-start(bf16[2,64,1152]{2,1,0:T(8,128)(2,1)S(1)} %all_to_all.85) | copy-start | bytes 884740
  766.8 0.6 copy-start.22
  785.2 18.2 %all-to-all-start.6 = ((bf16[1,1,2,64,8]{4,2,1,0,3:T(2,128)(2,1)}), bf16[1,1,2,64,8]{4,2,1,0,3:T(2,128)(2,1)}, u32[]{:S(2)}, u32[]{:S(2)}) async-start(bf16[1,1,2,64,8]{4,2,1,0,3:T(2,128)(2,1)} %copy.488), calls=%async_computation.6 | async-start | bytes 65536 | tf_op jit(solution)/shard_map/all_to_all | solution.py:127
  792.0 3.6 copy-start.23
  792.5 3.1 copy-start.8
  795.6 34.3 %copy-start.2 = (bf16[1,1,64,2,1,8,72]{6,5,4,2,3,1,0:T(8,128)(2,1)S(1)}, bf16[1,1,64,2,1,8,72]{6,5,4,2,3,1,0:T(8,128)(2,1)}, u32[]{:S(2)}) copy-start(bf16[1,1,64,2,1,8,72]{6,5,4,2,3,1,0:T(8,128)(2,1)} %copy-done.1) | copy-start | bytes 442372
  795.6 34.3 %copy-start.29 = (f32[8]{0:T(128)S(1)}, f32[8]{0:T(128)}, u32[]{:S(2)}) copy-start(f32[8]{0:T(128)} %get-tuple-element.42) | copy-start | bytes 100
  795.8 35.2 %copy-start.4 = (f32[2,8,64,64]{2,3,1,0:T(8,128)S(1)}, f32[2,8,64,64]{2,3,1,0:T(8,128)}, u32[]{:S(2)}) copy-start(f32[2,8,64,64]{2,3,1,0:T(8,128)} %copy-done.3) | copy-start | bytes 786436
  803.3 19.2 %all-to-all-start.4 = ((bf16[1,1,2,64,1152]{4,2,1,0,3:T(2,128)(2,1)}), bf16[1,1,2,64,1152]{4,2,1,0,3:T(2,128)(2,1)S(1)}, u32[]{:S(2)}, u32[]{:S(2)}) async-start(bf16[1,1,2,64,1152]{4,2,1,0,3:T(2,128)(2,1)} %copy.473), calls=%async_computation.4 | async-start | bytes 589824 | tf_op jit(solution)/shard_map/all_to_all | solution.py:126
  822.8 0.7 copy-start.11
  823.5 11.0 %copy-start.6 = (f32[1,1,64,2,8,72]{5,2,4,3,1,0:T(8,128)S(1)}, f32[1,1,64,2,8,72]{5,2,4,3,1,0:T(8,128)}, u32[]{:S(2)}) copy-start(f32[1,1,64,2,8,72]{5,2,4,3,1,0:T(8,128)} %get-tuple-element.46) | copy-start | bytes 884740
  836.6 12.4 %all-to-all-start.7 = ((bf16[8,2,128]{2,1,0:T(2,128)(2,1)}), bf16[8,2,128]{2,1,0:T(2,128)(2,1)S(1)}, u32[]{:S(2)}, u32[]{:S(2)}) async-start(bf16[8,2,128]{2,1,0:T(2,128)(2,1)} %reshape.584), calls=%async_computation.7 | async-start | bytes 8192 | tf_op jit(solution)/shard_map/all_to_all | solution.py:134
  844.1 3.6 copy-start.12
  844.1 3.6 copy-start.25
  847.7 18.3 %copy-start.27 = (f32[8]{0:T(128)S(1)}, f32[8]{0:T(128)}, u32[]{:S(2)}) copy-start(f32[8]{0:T(128)} %copy-done.26) | copy-start | bytes 100
  849.0 13.4 %all-to-all-start.5 = ((bf16[1,1,64,2,1152]{4,3,1,0,2:T(2,128)(2,1)}), bf16[1,1,64,2,1152]{4,3,1,0,2:T(2,128)(2,1)S(1)}, u32[]{:S(2)}, u32[]{:S(2)}) async-start(bf16[1,1,64,2,1152]{4,3,1,0,2:T(2,128)(2,1)} %copy.478), calls=%async_computation.5 | async-start | bytes 589824 | tf_op jit(solution)/shard_map/all_to_all | solution.py:133
  862.4 0.7 copy-start.9
  865.4 4.3 copy-start.5
  868.4 3.5 copy-start.20
  871.3 3.6 copy-start.10
  871.3 3.6 copy-start.18
Sparse Core Ops, SparseCore 0:
  12.1 153.9 all-gather.12
  170.0 91.1 all-gather.14
  264.6 145.9 all-gather.16
  413.9 91.1 all-gather.18
  508.3 90.7 all-gather.22
  602.4 145.9 all-gather.20
where the time goes:
time: 888 us; the launch traced here: 883 us
  waiting for transfers between devices  679 us (76%)
  local copies, waits for them, and re-layouts  86.3 us (10%)
  matrix products  53.3 us (6%)
  starting transfers between devices  45.9 us (5%)
  between operations  14.9 us (2%)
    all_gather x3, waiting for transfers between devices, weights_for(): lax.all_gather(w_qkv[sublayer], 'wa', axis=0, tiled=True)  433 us
    all_gather x3, waiting for transfers between devices, weights_for(): lax.all_gather(w_out[sublayer], 'wa', axis=0, tiled=True)  219 us
    all_gather x3, local copies, waits for them, and re-layouts, weights_for(): lax.all_gather(w_qkv[sublayer], 'wa', axis=0, tiled=True)  53.5 us
    dot_general x15, matrix products, product(): return jnp.einsum(form, left, right, preferred_element_type=jnp.float32)  18.4 us
  transfers between devices with their start and end apart: 14, of which 9 were waited for; matrix products, arithmetic and copies ran while one was open for 11% of the time, Pallas kernels for 0%

commit v1 on v0

v1 whole, which is shorter than its diff:
```python
import functools
import jax
import jax.numpy as jnp
from jax import lax
from jax.experimental import pallas as pl
from jax.experimental.pallas import tpu as pltpu
from jax.sharding import PartitionSpec as P

MESH = pl.DeviceIdType.MESH
QR, QC, OR, OC = 72, 896, 40, 640
BF = jnp.bfloat16
F32 = jnp.float32


def place():
    ha = lax.axis_index("ha")
    wa = lax.axis_index("wa")
    return ha // 2, ha % 2, wa // 8, (wa // 2) % 4, wa % 2


def gather_kernel(sq, so, gq, go, rq, ro, dq, do, lsem, zs, zr, ssem, rsem):
    zl, c, y, x, zh = place()
    ha = zl * 2 + c

    def dev(yy, xx):
        return (ha, (yy * 4 + xx) * 2 + zh)

    def along(d1, d2):
        dy = jnp.where(c == 0, d2, d1)
        dx = jnp.where(c == 0, d1, d2)
        return (y + dy + 4) % 4, (x + dx + 4) % 4

    def slot(d1, d2):
        yy, xx = along(d1, d2)
        return yy * 4 + xx

    ends = (zl == 0) | (zl == 3)
    near = 3 - zl
    far = jnp.where(zl == 3, 1, 2)
    zdev1 = (near * 2 + c, (y * 4 + x) * 2 + 1 - zh)
    zdev2 = (far * 2 + c, (y * 4 + x) * 2 + 1 - zh)
    zsrc_l = jnp.where(zl >= 2, 0, 3)
    zsrc = (zsrc_l * 2 + c, (y * 4 + x) * 2 + 1 - zh)
    sib = (zl * 2 + 1 - c, (y * 4 + x) * 2 + zh)
    p1 = {d: dev(*along(d, 0)) for d in (1, -1)}
    p2 = {d: dev(*along(0, d)) for d in (1, -1)}

    barrier = pltpu.get_barrier_semaphore()
    for t in (sib, p1[1], p1[-1], p2[1], p2[-1], zsrc):
        pl.semaphore_signal(barrier, inc=1, device_id=t, device_id_type=MESH)

    @pl.when(ends)
    def _():
        for t in (zdev1, zdev2):
            pl.semaphore_signal(barrier, inc=1, device_id=t, device_id_type=MESH)

    lq = pltpu.make_async_copy(sq.at[c], rq.at[zh], lsem.at[0])
    lo = pltpu.make_async_copy(so.at[c], ro.at[zh], lsem.at[1])
    lq.start()
    lo.start()
    pl.semaphore_wait(barrier, 6 + 2 * jnp.where(ends, 1, 0))

    def zcopy(src, dst, i, k, t):
        return pltpu.make_async_remote_copy(
            src_ref=src, dst_ref=dst, send_sem=zs.at[i, k], recv_sem=zr.at[k],
            device_id=t, device_id_type=MESH)

    @pl.when(ends)
    def _():
        for i, t in enumerate((zdev1, zdev2)):
            zcopy(sq.at[c], rq.at[zh], i, 0, t).start()
            zcopy(so.at[c], ro.at[zh], i, 1, t).start()

    lq.wait()
    lo.wait()
    zcopy(sq.at[c], rq.at[1 - zh], 0, 0, zdev1).wait_recv()
    zcopy(so.at[c], ro.at[1 - zh], 0, 1, zdev1).wait_recv()

    def perm(n, half, pad):
        r = lax.broadcasted_iota(jnp.int32, (n, 2 * pad), 0)
        k = lax.broadcasted_iota(jnp.int32, (n, 2 * pad), 1)
        want = jnp.where(r < half, r, jnp.where(r < 2 * half, r + pad - half, -1))
        return (k == want).astype(F32).astype(BF)

    pq = perm(QR, 36, 48)
    po = perm(OR, 18, 32)
    for l in range(3):
        dq[l] = jnp.dot(pq, rq[:, l].reshape(96, QC), preferred_element_type=F32).astype(BF)
        do[l] = jnp.dot(po, ro[:, l].reshape(64, OC), preferred_element_type=F32).astype(BF)

    sends = []
    n_send = [0]

    QP = ((0, 40), (40, 32))
    OP = ((0, 16), (16, 24))

    def qrows(half, s, part):
        o, n = (0, QR) if part is None else QP[part]
        return gq.at[half, :, pl.ds(pl.multiple_of(s * QR + o, 8), n), :]

    def orows(half, s, part):
        o, n = (0, OR) if part is None else OP[part]
        return go.at[half, :, pl.ds(pl.multiple_of(s * OR + o, 8), n), :]

    def send(s, part, r, t, own=False, half=None):
        half = c if half is None else half
        for k, (rows, d) in enumerate(((qrows, dq), (orows, do))):
            cp = pltpu.make_async_remote_copy(
                src_ref=d if own else rows(half, s, part), dst_ref=rows(half, s, part),
                send_sem=ssem.at[n_send[0], k], recv_sem=rsem.at[r, k],
                device_id=t, device_id_type=MESH)
            cp.start()
            sends.append(cp)
        n_send[0] += 1

    def recv(s, part, r, half=None):
        half = c if half is None else half
        for k, rows in enumerate((qrows, orows)):
            pltpu.make_async_remote_copy(
                src_ref=rows(half, s, part), dst_ref=rows(half, s, part),
                send_sem=ssem.at[0, k], recv_sem=rsem.at[r, k],
                device_id=sib, device_id_type=MESH).wait_recv()

    def m2(b, k):
        return 4 + 4 * b + k

    own = slot(0, 0)
    lq2 = pltpu.make_async_copy(dq, qrows(c, own, None), lsem.at[0])
    lo2 = pltpu.make_async_copy(do, orows(c, own, None), lsem.at[1])
    D1 = (0, -1, 1, 2)

    def sibling(i, j, s, own=False):
        send(s, None, 20 + 4 * i + j, sib, own=own)

    send(own, None, 0, p1[1], own=True)
    send(own, None, 1, p1[-1], own=True)
    send(own, None, m2(0, 0), p2[1], own=True)
    send(own, None, m2(0, 1), p2[-1], own=True)
    lq2.start()
    lo2.start()
    sibling(0, 0, own, own=True)
    for b, d in ((1, -1), (2, 1)):
        s = slot(d, 0)
        recv(s, None, b - 1)
        send(s, b - 1, 2 + (b - 1), p1[-d])
        send(s, None, m2(b, 0), p2[1])
        send(s, None, m2(b, 1), p2[-1])
        sibling(b, 0, s)
    s = slot(2, 0)
    recv(s, 0, 2)
    recv(s, 1, 3)
    send(s, None, m2(3, 0), p2[1])
    send(s, None, m2(3, 1), p2[-1])
    sibling(3, 0, s)
    for b, d in enumerate(D1):
        for k, e in ((0, -1), (1, 1)):
            s = slot(d, e)
            recv(s, None, m2(b, k))
            send(s, k, m2(b, 2 + k), p2[-e])
            sibling(b, 1 + k, s)
    for b, d in enumerate(D1):
        s = slot(d, 2)
        recv(s, 0, m2(b, 2))
        recv(s, 1, m2(b, 3))
        sibling(b, 3, s)
    lq2.wait()
    lo2.wait()
    for i, d in enumerate(D1):
        for j, e in enumerate((0, -1, 1, 2)):
            recv(slot(e, d), None, 20 + 4 * i + j, half=1 - c)
    for cp in sends:
        cp.wait_send()

    @pl.when(ends)
    def _():
        for i, t in enumerate((zdev1, zdev2)):
            zcopy(sq.at[c], rq.at[zh], i, 0, t).wait_send()
            zcopy(so.at[c], ro.at[zh], i, 1, t).wait_send()


def gather(sq, so):
    return pl.pallas_call(
        gather_kernel,
        out_shape=(jax.ShapeDtypeStruct((2, 3, 1152, QC), BF), jax.ShapeDtypeStruct((2, 3, 640, OC), BF)),
        in_specs=[pl.BlockSpec(memory_space=pl.ANY)] * 2,
        out_specs=(pl.BlockSpec(memory_space=pl.ANY),) * 2,
        scratch_shapes=[
            pltpu.VMEM((2, 3, 48, QC), BF), pltpu.VMEM((2, 3, 32, OC), BF),
            pltpu.VMEM((3, QR, QC), BF), pltpu.VMEM((3, OR, OC), BF),
            pltpu.SemaphoreType.DMA((2,)),
            pltpu.SemaphoreType.DMA((2, 2)), pltpu.SemaphoreType.DMA((2,)),
            pltpu.SemaphoreType.DMA((36, 2)), pltpu.SemaphoreType.DMA((36, 2)),
        ],
        compiler_params=pltpu.CompilerParams(collective_id=0, has_side_effects=True),
        name="weights",
    )(sq, so)


def shard_halves(w_qkv, w_out):
    v = jnp.pad(w_qkv[..., 1152:].reshape(3, 36, 16, 36), ((0, 0), (0, 0), (0, 0), (0, 4))).reshape(3, 36, 640)
    q = jnp.concatenate([w_qkv[..., :1152], v], axis=-1)
    q = jnp.pad(q, ((0, 0), (0, 12), (0, 0)))
    o = jnp.pad(w_out, ((0, 0), (0, 14), (0, 128)))
    return (jnp.stack([q[..., :896], q[..., 896:]]), jnp.stack([o[..., :640], o[..., 640:]]))


SCALE = 72 ** (-0.5)
HEADS = 8


def dot(a, b):
    return jnp.dot(a, b, preferred_element_type=F32)


def dot_nt(a, b):
    return lax.dot_general(a, b, (((1,), (1,)), ((), ())), preferred_element_type=F32)


def dot_tn(a, b):
    return lax.dot_general(a, b, (((0,), (0,)), ((), ())), preferred_element_type=F32)


def window(h, width):
    lo = (width * h) // 128 * 128
    hi = -(-(width * (h + 1)) // 128) * 128
    return lo, hi


def lanes(h, width):
    lo, hi = window(h, width)
    i = lax.broadcasted_iota(jnp.int32, (1, hi - lo), 1) + lo
    return ((i >= width * h) & (i < width * (h + 1))).astype(F32).astype(BF)


class Tiles:
    def __init__(self):
        self.t = [None] * 5

    def add(self, lo, value):
        for n in range(value.shape[1] // 128):
            part = value[:, 128 * n:128 * (n + 1)]
            at = lo // 128 + n
            self.t[at] = part if self.t[at] is None else self.t[at] + part

    def all(self):
        return jnp.concatenate(self.t, axis=1)


def same_line(layer):
    r = lax.broadcasted_iota(jnp.int32, (128, 128), 0)
    k = lax.broadcasted_iota(jnp.int32, (128, 128), 1)
    if layer == 0:
        return (r % 16) == (k % 16)
    if layer == 1:
        return (r % 2) == (k % 2)
    return ((r // 2) % 2) == ((k // 2) % 2)


def spread(second):
    r = lax.broadcasted_iota(jnp.int32, (256, 128), 0)
    k = lax.broadcasted_iota(jnp.int32, (256, 128), 1)
    r8 = r % 8
    want = (r // 8) * 4 + r8 - (4 if second else 0)
    ok = (r8 >= 4) if second else (r8 < 4)
    return ((k == want) & ok).astype(F32).astype(BF)


def collect(second):
    r = lax.broadcasted_iota(jnp.int32, (128, 256), 0)
    k = lax.broadcasted_iota(jnp.int32, (128, 256), 1)
    return (k == (r // 4) * 8 + r % 4 + (4 if second else 0)).astype(F32).astype(BF)


def pack(ref, x, y):
    s = dot(spread(False), x) + dot(spread(True), y)
    ref[...] = s.reshape(32, 8, 640).astype(BF)


def unpack(ref):
    r = ref[...].astype(F32).reshape(256, 640).astype(BF)
    a = dot(collect(False), r)
    b = dot(collect(True), r)
    return jnp.concatenate([a, b[:, 128:]], axis=1).astype(BF), b[:, :128].astype(BF)


class Net:
    def __init__(self, ssem, rsem):
        self.ha = lax.axis_index("ha")
        self.wa = lax.axis_index("wa")
        self.ssem, self.rsem = ssem, rsem

    def barrier(self):
        b = pltpu.get_barrier_semaphore()

        def ha(k, u):
            pl.semaphore_signal(b, inc=1, device_id=((self.ha + k) % 8, self.wa), device_id_type=MESH)
            return u

        def wa(k, u):
            pl.semaphore_signal(b, inc=1, device_id=(self.ha, (self.wa + k) % 32), device_id_type=MESH)
            return u

        lax.fori_loop(1, 8, ha, 0)
        lax.fori_loop(1, 32, wa, 0)
        pl.semaphore_wait(b, 38)

    def send_ha(self, n, src, dst):
        me = pl.ds(pl.multiple_of(self.ha * 16, 16), 16)

        def one(k, u):
            j = (self.ha + k) % 8
            pltpu.make_async_remote_copy(
                src_ref=src.at[pl.ds(pl.multiple_of(j * 16, 16), 16)], dst_ref=dst.at[me],
                send_sem=self.ssem.at[n], recv_sem=self.rsem.at[n],
                device_id=(j, self.wa), device_id_type=MESH).start()
            return u

        lax.fori_loop(1, 8, one, 0)
        dst[me] = src[me]

    def send_wa(self, n, src, dst):
        def one(k, u):
            j = (self.wa + k) % 32
            pltpu.make_async_remote_copy(
                src_ref=src.at[j], dst_ref=dst.at[self.wa],
                send_sem=self.ssem.at[n], recv_sem=self.rsem.at[n],
                device_id=(self.ha, j), device_id_type=MESH).start()
            return u

        lax.fori_loop(1, 32, one, 0)
        dst[self.wa] = src[self.wa]

    def wait(self, sems, n, ref):
        part = ref.at[pl.ds(0, 112)] if ref.shape[0] == 128 else ref.at[pl.ds(0, 31)]
        pltpu.make_async_copy(part, part, sems.at[n]).wait()


def step_kernel(x0, cot, gq, go, gains, gates, grad, sens,
                wq, wo, q_s, k_s, v_s, a_s, p_s, x1s, x1, c1, cs, cr, x2s, x2r, g2s, g2r, g1s, g1r,
                wsem, ssem, rsem):
    net = Net(ssem, rsem)
    loads = []
    for l in range(3):
        cps = [pltpu.make_async_copy(gq.at[c, l], wq.at[c, l], wsem.at[l, c]) for c in range(2)]
        cps += [pltpu.make_async_copy(go.at[c, l], wo.at[c, l], wsem.at[l, 2 + c]) for c in range(2)]
        for cp in cps:
            cp.start()
        loads.append(cps)
    net.barrier()
    net.send_ha(0, cot, c1)

    def norm(x):
        xf = x.astype(F32)
        return xf, lax.rsqrt(jnp.mean(xf * xf, axis=-1, keepdims=True) + 1e-06)

    def forward(l, x):
        gain = gains[l:l + 1, :]
        xf, inv = norm(x)
        normed = (xf * inv * gain).astype(BF)
        a = dot(normed, wq[0, l])
        b = dot(normed, wq[1, l])
        q_s[l] = a[:, :640].astype(BF)
        k_s[l] = pltpu.roll(jnp.concatenate([a[:, 512:], b[:, :256]], axis=1), 576, 1).astype(BF)
        v_s[l] = b[:, 256:].astype(BF)
        line = same_line(l)
        att = Tiles()
        for h in range(HEADS):
            lo, hi = window(h, 72)
            s = dot_nt(q_s[l, :, lo:hi] * lanes(h, 72), k_s[l, :, lo:hi]) * SCALE
            e = jnp.where(line, jnp.exp(s), 0.0)
            p = e / jnp.sum(e, axis=-1, keepdims=True)
            p_s[l, h] = p
            lo, hi = window(h, 80)
            att.add(lo, dot(p.astype(BF), v_s[l, :, lo:hi] * lanes(h, 80)))
        a_s[l] = att.all().astype(BF)

    def output(l, x):
        gated = (a_s[l].astype(F32) * gates[l:l + 1, :]).astype(BF)
        o = jnp.concatenate([dot(gated, wo[0, l]), dot(gated, wo[1, l, :, :512])], axis=1)
        return (x.astype(F32) + o).astype(BF)

    def dgated_of(l, og):
        return (dot_nt(og[:, :640], wo[0, l]) + dot_nt(og[:, 640:], wo[1, l, :, :512])).astype(BF)

    def backward(l, og, x, dg):
        gain = gains[l:l + 1, :]
        prod = dg.astype(F32) * a_s[l].astype(F32)
        high = prod.astype(BF)
        low = (prod - high.astype(F32)).astype(BF)
        i = lax.broadcasted_iota(jnp.int32, (640, 128), 0)
        k = lax.broadcasted_iota(jnp.int32, (640, 128), 1)
        pick = ((i >= 80 * (k - 8 * l)) & (i < 80 * (k - 8 * l) + 80)).astype(F32).astype(BF)
        sn = dot(high, pick) + dot(low, pick)
        da = (dg.astype(F32) * gates[l:l + 1, :]).astype(BF)
        dq, dk, dv = Tiles(), Tiles(), Tiles()
        for h in range(HEADS):
            lo, hi = window(h, 80)
            p = p_s[l, h]
            dah = da[:, lo:hi] * lanes(h, 80)
            dp = dot_nt(dah, v_s[l, :, lo:hi])
            dv.add(lo, dot_tn(p.astype(BF), dah))
            ds = (p * (dp - jnp.sum(dp * p, axis=-1, keepdims=True)) * SCALE).astype(BF)
            lo, hi = window(h, 72)
            m = lanes(h, 72)
            dq.add(lo, dot(ds, k_s[l, :, lo:hi] * m))
            dk.add(lo, dot_tn(ds, q_s[l, :, lo:hi] * m))
        dqv = dq.all()
        dkv = pltpu.roll(dk.all(), 64, 1)
        dqk = jnp.concatenate([dqv[:, :512], dqv[:, 512:] + dkv[:, :128], dkv[:, 128:]], axis=1)
        d0 = dqk[:, :896].astype(BF)
        d1 = jnp.concatenate([dqk[:, 896:], dv.all()], axis=1).astype(BF)
        dn = (dot_nt(d0, wq[0, l]) + dot_nt(d1, wq[1, l])) * gain
        xf, inv = norm(x)
        g = og.astype(F32) + inv * dn - xf * inv * inv * inv * jnp.mean(xf * dn, axis=-1, keepdims=True)
        return g.astype(BF), sn

    for cp in loads[0]:
        cp.wait()
    forward(0, x0[...])
    x1s[...] = output(0, x0[...])
    net.send_ha(1, x1s, x1)

    net.wait(rsem, 0, c1)
    pack(cs, c1[:, :640], c1[:, 512:])
    net.send_wa(2, cs, cr)
    for cp in loads[1]:
        cp.wait()
    net.wait(rsem, 1, x1)
    forward(1, x1[...])
    o1 = output(1, x1[...])
    pack(x2s, o1[:, :640], o1[:, 512:])
    net.send_wa(3, x2s, x2r)
    for cp in loads[2]:
        cp.wait()
    net.wait(rsem, 2, cr)
    og2, _ = unpack(cr)
    dg2 = dgated_of(2, og2)
    net.wait(rsem, 3, x2r)
    xx2, _ = unpack(x2r)
    forward(2, xx2)
    g2, sn2 = backward(2, og2, xx2, dg2)
    pack(g2s, g2[:, :640], jnp.concatenate([sn2.astype(BF), g2[:, 640:]], axis=1))
    net.send_wa(4, g2s, g2r)
    net.wait(rsem, 4, g2r)
    og1, sn2h = unpack(g2r)
    g1, sn1 = backward(1, og1, x1[...], dgated_of(1, og1))
    g1s[:, :1152] = g1
    g1s[:, 1152:] = (sn1 + sn2h.astype(F32)).astype(BF)
    net.send_ha(5, g1s, g1r)
    net.wait(rsem, 5, g1r)
    og0 = g1r[:, :1152]
    g0, sn0 = backward(0, og0, x0[...], dgated_of(0, og0))
    grad[...] = g0
    sens[...] = (sn0 + g1r[:, 1152:].astype(F32)).astype(BF)
    for n, ref in ((0, c1), (1, x1), (2, cr), (3, x2r), (4, g2r), (5, g1r)):
        net.wait(ssem, n, ref)


def steps(x, cot, gq, go, gains, gates):
    vm = pl.BlockSpec(memory_space=pltpu.VMEM)
    hb = pl.BlockSpec(memory_space=pl.ANY)
    tok = lambda n: pltpu.VMEM((128, n), BF)
    slots = pltpu.VMEM((32, 8, 640), BF)
    per = lambda: pltpu.VMEM((3, 128, 640), BF)
    return pl.pallas_call(
        step_kernel,
        out_shape=(jax.ShapeDtypeStruct((128, 1152), BF), jax.ShapeDtypeStruct((128, 128), BF)),
        in_specs=[vm, vm, hb, hb, vm, vm],
        out_specs=(vm, vm),
        scratch_shapes=[
            pltpu.VMEM((2, 3, 1152, 896), BF), pltpu.VMEM((2, 3, 640, 640), BF),
            per(), per(), per(), per(), pltpu.VMEM((3, HEADS, 128, 128), F32),
            tok(1152), tok(1152), tok(1152), slots, slots, slots, slots, slots, slots, tok(1280), tok(1280),
            pltpu.SemaphoreType.DMA((3, 4)), pltpu.SemaphoreType.DMA((6,)), pltpu.SemaphoreType.DMA((6,)),
        ],
        compiler_params=pltpu.CompilerParams(collective_id=1, has_side_effects=True, vmem_limit_bytes=60 << 20),
        name="steps",
    )(x, cot, gq, go, gains, gates)


def per_device(tokens, cotangent, w_qkv, w_out, gains, gates):
    gq, go = gather(*shard_halves(w_qkv, w_out))
    wide = jnp.repeat(gates, 80, axis=1)
    grad, sens = steps(tokens.reshape(128, 1152), cotangent.reshape(128, 1152), gq, go, gains, wide)
    head_sens = sens[:, :24].reshape(8, 8, 2, 3, 8).transpose(3, 0, 1, 2, 4)[None]
    return (grad.reshape(tokens.shape), head_sens)


def solution(mesh):
    in_specs = (
        P(None, None, "ha", "wa", None),
        P(None, None, "ha", "wa", None),
        P(None, "wa", None),
        P(None, "wa", None),
        P(),
        P(),
    )
    out_specs = (P(None, None, "ha", "wa", None), P(None, None, None, "ha", "wa", None))
    return jax.shard_map(
        per_device, mesh=mesh, in_specs=in_specs, out_specs=out_specs, check_vma=False
    )
```

time: 888 us -> 165 us (0.19)
  waiting for transfers between devices: 679 us -> 0 us
  Pallas kernels: 0 us -> 149 us
  local copies, waits for them, and re-layouts: 86.3 us -> 12.5 us
  matrix products: 53.3 us -> 0 us
  starting transfers between devices: 45.9 us -> 0 us
  between operations: 14.9 us -> 0.7 us
    all_gather x6 -> x0, waiting for transfers between devices: 652 us -> none  [the longest x3 433 us: weights_for(): lax.all_gather(w_qkv[sublayer], 'wa', axis=0, tiled=True)]
    pallas_call x0 -> x2, Pallas kernels: none -> 149 us  [the longest x1 76 us: gather(): pl.pallas_call(gather_kernel, out_shape=(jax.ShapeDtypeStruct((2, 3, 1152...]
    all_gather x3 -> x0, local copies, waits for them, and re-layouts: 53.5 us -> none  [weights_for(): lax.all_gather(w_qkv[sublayer], 'wa', axis=0, tiled=True)]
    dot_general x26 -> x0, matrix products: 51.2 us -> none  [the longest x15 18.4 us: product(): return jnp.einsum(form, left, right, preferred_element_type=jnp.float32)]
    all_to_all x8 -> x0, starting transfers between devices: 45.7 us -> none  [the longest x1 6.83 us: per_device(): lax.all_to_all(jnp.concatenate([tall_sens, sens_height], axis=-1), 'ha',...]
    all_to_all x8 -> x0, waiting for transfers between devices: 27 us -> none  [the longest x1 12.6 us: per_device(): lax.all_to_all(grad_width, 'wa', split_axis=3, concat_axis=2, tiled=True)]
    convert_element_type x16 -> x0, local copies, waits for them, and re-layouts: 11.7 us -> none  [the longest x6 5.03 us: backward_sublayer(): d_gated.astype(jnp.float32) * gate[:, None]]
  transfers between devices with their start and end apart: 14 -> 0, of which waited for: 9 -> 0; matrix products, arithmetic and copies ran while one was open for 11% -> 0% of each run, Pallas kernels for 0% -> 0%
where the time goes in v1:
time: 165 us; the launch traced here: 163 us
  Pallas kernels  149 us (90%)
  local copies, waits for them, and re-layouts  12.5 us (8%)
    pallas_call x1, Pallas kernels, gather(): pl.pallas_call(gather_kernel, out_shape=(jax.ShapeDtypeStruct((2, 3, 1152...  76 us
    pallas_call x1, Pallas kernels, steps(): pl.pallas_call(step_kernel, out_shape=(jax.ShapeDtypeStruct((128, 1152),...  72.6 us

profile of v1, /device:TPU:32, one launch (start us, length us, event | category | flops | bytes accessed | tf_op | source)
XLA Modules:
  0.0 163.4 jit_solution(9243765352253336825)
XLA Ops:
  0.6 0.9 slice.22
  1.6 0.7 reshape.27
  2.2 0.1 pad.12
  2.3 0.5 reshape.28
  2.8 1.0 slice.21
  3.9 0.8 pad_maximum_fusion.sq
  4.7 0.9 fusion.3
  5.7 0.7 pad_maximum_fusion.1.so
  6.4 76.0 %weights.1 = (bf16[2,3,1152,896]{3,2,1,0:T(8,128)(2,1)}, bf16[2,3,640,640]{3,2,1,0:T(8,128)(2,1)}) custom-call(bf16[2,3,48,896]{3,2,1,0:T(8,128)(2,1)} %pad_maximum_fusion.sq, bf16[2,3,32,640]{3,2,1,0:T(8,128)(2,1)} %pad_maximum_fusion.1.so), custom_call_target="tpu_custom_call" | custom-call | tf_op jit(solution)/shard_map/weights/pallas_call | solution.py:182
  82.4 1.8 %reshape.25.x0 = bf16[128,1152]{1,0:T(8,128)(2,1)} reshape(bf16[1,8,8,2,1152]{4,3,2,1,0:T(2,128)(2,1)} %param.6) | data formatting | bytes 589824 | tf_op jit(solution)/shard_map/reshape | solution.py:484
  84.2 1.8 %reshape.26.cot = bf16[128,1152]{1,0:T(8,128)(2,1)} reshape(bf16[1,8,8,2,1152]{4,3,2,1,0:T(2,128)(2,1)} %param.7) | data formatting | bytes 589824 | tf_op jit(solution)/shard_map/reshape | solution.py:484
  85.9 0.8 broadcast_in_dim.6
  86.7 0.7 reshape.29.gates
  87.4 72.6 %steps.1 = (bf16[128,1152]{1,0:T(8,128)(2,1)}, bf16[128,128]{1,0:T(8,128)(2,1)}) custom-call(bf16[128,1152]{1,0:T(8,128)(2,1)} %reshape.25.x0, bf16[128,1152]{1,0:T(8,128)(2,1)} %reshape.26.cot, bf16[2,3,1152,896]{3,2,1,0:T(8,128)(2,1)} %get-tuple-element.6.gq, bf16[2,3,640,640]{3,2,1,0:T(8,128)(2,1)} %get-tuple-element.7.go, f32[3,1152]{1,0:T(4,128)} %gains.1, ...), custom_call_target="tpu_custom_call" | custom-call | tf_op jit(solution)/shard_map/steps/pallas_call | solution.py:465
  160.0 1.8 %reshape.30 = bf16[1,8,8,2,1152]{4,3,2,1,0:T(2,128)(2,1)} reshape(bf16[128,1152]{1,0:T(8,128)(2,1)} %get-tuple-element.8) | data formatting | bytes 589824 | tf_op jit(solution)/shard_map/reshape | solution.py:486
  161.8 0.9 reshape.31
  162.6 0.7 copy.9
  (2 shorter events, 0.1 us)
